TPU v7x, 256 devices: a whole 4x4x8 slice. The times are simulated.
256 devices in a mesh: pb: 16 (over z, core), kv: 16 (over y, x).
Axes of the slice: x: 4, y: 4, z: 8, core: 2. Of those that a mesh axis runs over, the one named last changes fastest.
Arguments:
- queries: bfloat16 [393216, 1024], P(('pb', 'kv')), may hold values from -8 to 8
- keys: bfloat16 [524288, 128], P(('kv', 'pb')), may hold values from -6 to 6
- values: bfloat16 [524288, 128], P(('kv', 'pb')), may hold values from -6 to 6
- selected: int32 [6144, 14], P(('pb', 'kv')), may hold values from 1 to 8190, as said below
Outputs:
- attended: bfloat16 [393216, 1024], P(('pb', 'kv'))
Inputs may be any that keep to these rules, and one draw needn't show every extreme that they name: `selected`: each row names 14 different blocks, never block 0 or block 8191. Key device k holds blocks k * 32 to (k + 1) * 32 - 1, devices counted with kv slowest; query device d holds query blocks d * 24 to (d + 1) * 24 - 1, devices counted with pb slowest. The query blocks of one device name together at most 2 distinct blocks of one key device, and in every draw some key device has exactly 2 named by every query device.
All inputs are finite; a program needn't handle non-finite values.
Results may differ from a plain program's by a relative error of at most 0.0046.
Values may be sent and summed in bfloat16 or wider, within the bound.
A program may use at most 128 MiB of HBM per device.

v0:
```python
import math
import jax
import jax.numpy as jnp
from jax import lax
from jax.sharding import PartitionSpec as P

H = 8
DH = 128
BLOCK = 64
TOPN = 16
QB = 64
CAP = 2


def holdings(wanted, owner, blocks_here):
    local_ids = owner * blocks_here + jnp.arange(blocks_here, dtype=jnp.int32)
    hits = (wanted[:, None] == local_ids[None, :]).astype(jnp.int32)
    present = jnp.max(hits, axis=0)
    return (present, jnp.cumsum(present) - present)


def slot_lists(present, slot_rank, slots):
    local_ids = jnp.arange(present.shape[-1], dtype=jnp.int32)
    slot_ids = jnp.arange(slots, dtype=jnp.int32)
    matches = (present[..., :, None] == 1) & (slot_rank[..., :, None] == slot_ids)
    return jnp.sum(jnp.where(matches, local_ids[:, None], 0), axis=-2)


def per_device(queries, keys, values, selected):
    pb_count = lax.axis_size("pb")
    kv_count = lax.axis_size("kv")
    devices = pb_count * kv_count
    blocks_here = keys.shape[0] // BLOCK
    query_blocks = queries.shape[0] // QB
    column_blocks = pb_count * blocks_here
    tiles_local = jnp.concatenate(
        [keys.reshape(blocks_here, BLOCK, DH), values.reshape(blocks_here, BLOCK, DH)], axis=2
    )
    column = lax.all_gather(tiles_local, "pb", axis=0, tiled=True)
    slots = CAP
    wanted = selected.reshape(-1)
    owners = jnp.arange(devices, dtype=jnp.int32)
    present, slot_rank = jax.vmap(lambda owner: holdings(wanted, owner, blocks_here))(owners)
    owner_lists = slot_lists(present, slot_rank, slots)
    by_column = (
        owner_lists.reshape(kv_count, pb_count, slots)
        + jnp.arange(pb_count, dtype=jnp.int32)[None, :, None] * blocks_here
    )
    by_column = by_column.reshape(kv_count, pb_count * slots)
    asked_for = lax.all_to_all(by_column, "kv", split_axis=0, concat_axis=0, tiled=True)
    me_kv = lax.axis_index("kv")
    end_pick = jnp.where(me_kv == kv_count - 1, column_blocks - 1, 0).astype(jnp.int32)
    picks = jnp.concatenate(
        [asked_for.reshape(kv_count, pb_count * slots), jnp.broadcast_to(end_pick, (kv_count, 1))],
        axis=1,
    )
    outgoing = jnp.take(column, picks.reshape(-1), axis=0).reshape(
        kv_count, pb_count * slots + 1, BLOCK, 2 * DH
    )
    fetched = lax.all_to_all(outgoing, "kv", split_axis=0, concat_axis=0, tiled=True)
    tile_table = fetched.reshape(devices * slots + kv_count, BLOCK, 2 * DH)
    owner_of = selected // blocks_here
    positions = owner_of * slots + jnp.take(slot_rank.reshape(-1), selected)
    positions = positions + owner_of // pb_count
    row = pb_count * slots + 1
    leading_positions = jnp.broadcast_to(
        jnp.array([row - 1, kv_count * row - 1], jnp.int32), (query_blocks, 2)
    )
    positions = jnp.concatenate([leading_positions, positions], axis=1)
    group_size = math.gcd(query_blocks, 8)
    q_groups = queries.reshape(query_blocks // group_size, group_size, QB * H, DH)
    p_groups = positions.reshape(query_blocks // group_size, group_size, TOPN)

    def attend(operands):
        q_block, positions_in = operands
        gathered = jnp.take(tile_table, positions_in.reshape(-1), axis=0).reshape(
            group_size, TOPN * BLOCK, 2 * DH
        )
        scores = jnp.einsum(
            "gqd,gkd->gqk", q_block, gathered[..., :DH], preferred_element_type=jnp.float32
        ) * DH ** (-0.5)
        weights = jnp.exp(scores - jnp.max(scores, axis=-1, keepdims=True))
        totals = jnp.sum(weights, axis=-1, keepdims=True)
        weighted = jnp.einsum(
            "gqk,gkd->gqd",
            weights.astype(jnp.bfloat16),
            gathered[..., DH:],
            preferred_element_type=jnp.float32,
        )
        return (weighted / totals).astype(jnp.bfloat16)

    result = lax.map(attend, (q_groups, p_groups))
    return result.reshape(query_blocks * QB, H * DH)


def solution(mesh):
    placed = (
        P(("pb", "kv"), None),
        P(("kv", "pb"), None),
        P(("kv", "pb"), None),
        P(("pb", "kv"), None),
    )
    return jax.shard_map(
        per_device, mesh=mesh, in_specs=placed, out_specs=P(("pb", "kv"), None), check_vma=False
    )
```

profile of v0, /device:TPU:1, one launch (start us, length us, event | category | flops | bytes accessed | tf_op | source)
XLA Modules:
  0.0 494.0 jit_solution(9905077446433948110)
XLA Ops:
  6.5 2.3 pad_maximum_fusion
  8.9 0.8 copy.30
  9.8 1.7 convert_reduce_fusion
  11.6 0.1 copy.38
  11.8 0.1 reshape.199
  12.1 0.6 broadcast_add_fusion
  12.7 7.6 %all-to-all-start = ((s32[16,1,32]{2,1,0:T(1,128)}), s32[16,1,32]{2,1,0:T(1,128)S(1)}, u32[]{:S(2)}, u32[]{:S(2)}) async-start(s32[16,1,32]{2,1,0:T(1,128)} %bitcast.6), calls=%async_computation | async-start | bytes 16384 | tf_op jit(solution)/shard_map/all_to_all | solution.py:50
  20.3 6.4 %all-to-all-done = s32[16,1,32]{2,1,0:T(1,128)S(1)} async-done(((s32[16,1,32]{2,1,0:T(1,128)}), s32[16,1,32]{2,1,0:T(1,128)S(1)}, u32[]{:S(2)}, u32[]{:S(2)}) %all-to-all-start) | async-done | bytes 2080 | tf_op jit(solution)/shard_map/all_to_all | solution.py:50
  26.8 82.0 %all-gather.2.cloned.1.call-done = bf16[512,64,256]{2,1,0:T(8,128)(2,1)} async-done(((bf16[32,64,256]{2,1,0:T(8,128)(2,1)}), bf16[512,64,256]{2,1,0:T(8,128)(2,1)}) %all-gather.2.cloned.1.call-update) | async-done | bytes 16777232 | tf_op jit(solution)/shard_map/all_gather | solution.py:39
  108.9 21.2 %gather_fusion.2 = bf16[528,64,256]{2,1,0:T(8,128)(2,1)} fusion(bf16[512,64,256]{2,1,0:T(8,128)(2,1)} %all-gather.2.cloned.1.call-done, s32[1024]{0:T(1024)S(1)} %pad_clamp_fusion.1), kind=kCustom, calls=%fused_computation.2 | custom fusion | bytes 34605120 | tf_op jit(solution)/shard_map/jit(_take)/gather | solution.py:57
  130.1 14.4 %broadcast_select_fusion = bf16[16,33,64,256]{3,2,1,0:T(8,128)(2,1)} fusion(bf16[16,33,64,256]{3,2,1,0:T(8,128)(2,1)} %bitcast.37, pred[16,33]{1,0:T(8,128)(4,1)S(1)} %compare_and_fusion.1), kind=kLoop, calls=%fused_computation.26 | loop fusion | flops 8650752 | bytes 34603536 | tf_op jit(solution)/shard_map/jit(_take)/select_n | solution.py:57
  144.5 6.6 %all-to-all-start.1 = ((bf16[16,33,64,256]{3,2,1,0:T(8,128)(2,1)}), bf16[16,33,64,256]{3,2,1,0:T(8,128)(2,1)}, u32[]{:S(2)}, u32[]{:S(2)}) async-start(bf16[16,33,64,256]{3,2,1,0:T(8,128)(2,1)} %broadcast_select_fusion), calls=%async_computation.1 | async-start | bytes 34603008 | tf_op jit(solution)/shard_map/all_to_all | solution.py:60
  151.5 2.5 gather_fusion.1
  154.1 4.1 reshape.197
  158.4 251.6 %all-to-all-done.1 = bf16[16,33,64,256]{3,2,1,0:T(8,128)(2,1)} async-done(((bf16[16,33,64,256]{3,2,1,0:T(8,128)(2,1)}), bf16[16,33,64,256]{3,2,1,0:T(8,128)(2,1)}, u32[]{:S(2)}, u32[]{:S(2)}) %all-to-all-start.1) | async-done | bytes 17301536 | tf_op jit(solution)/shard_map/all_to_all | solution.py:60
  410.0 71.4 %while.10 = (s32[]{:T(128)}, bf16[3,8,512,128]{3,2,1,0:T(8,128)(2,1)}, bf16[3,8,512,128]{3,2,1,0:T(8,128)(2,1)S(1)}, s32[3,8,16]{2,1,0:T(8,128)S(1)}, bf16[528,64,256]{2,1,0:T(8,128)(2,1)}, /*index=5*/s32[]{:T(128)}) while((s32[]{:T(128)}, bf16[3,8,512,128]{3,2,1,0:T(8,128)(2,1)}, bf16[3,8,512,128]{3,2,1,0:T(8,128)(2,1)S(1)}, ...), condition=%wide.region_6.7_spmd, body=%wide.region_3.6_spmd.sunk | while | flops 2184177664 | bytes 73524040 | solution.py:92
  410.1 8.7 %gather_fusion = bf16[128,64,256]{2,1,0:T(8,128)(2,1)} fusion(bf16[528,64,256]{2,1,0:T(8,128)(2,1)} %get-tuple-element.102, s32[1024]{0:T(1024)S(1)} %pad_clamp_fusion.4), kind=kCustom, calls=%fused_computation.clone.1 | custom fusion | bytes 8389120 | tf_op jit(solution)/shard_map/while/body/eval_jaxpr/jit(_take)/gather | solution.py:76
  419.0 4.6 bitcast_select_fusion.2
  423.6 2.4 multiply_reduce_fusion.2
  426.0 3.5 fusion.32
  429.5 4.3 bitcast_dynamic-update-slice_fusion.2
  433.9 8.7 %gather_fusion = bf16[128,64,256]{2,1,0:T(8,128)(2,1)} fusion(bf16[528,64,256]{2,1,0:T(8,128)(2,1)} %get-tuple-element.102, s32[1024]{0:T(1024)S(1)} %pad_clamp_fusion.4), kind=kCustom, calls=%fused_computation.clone.1 | custom fusion | bytes 8389120 | tf_op jit(solution)/shard_map/while/body/eval_jaxpr/jit(_take)/gather | solution.py:76
  442.8 4.6 bitcast_select_fusion.2
  447.4 2.4 multiply_reduce_fusion.2
  449.8 3.5 fusion.32
  453.3 4.2 bitcast_dynamic-update-slice_fusion.2
  457.7 8.7 %gather_fusion = bf16[128,64,256]{2,1,0:T(8,128)(2,1)} fusion(bf16[528,64,256]{2,1,0:T(8,128)(2,1)} %get-tuple-element.102, s32[1024]{0:T(1024)S(1)} %pad_clamp_fusion.4), kind=kCustom, calls=%fused_computation.clone.1 | custom fusion | bytes 8389120 | tf_op jit(solution)/shard_map/while/body/eval_jaxpr/jit(_take)/gather | solution.py:76
  466.6 4.6 bitcast_select_fusion.2
  471.1 2.4 multiply_reduce_fusion.2
  473.6 3.5 fusion.32
  477.1 4.2 bitcast_dynamic-update-slice_fusion.2
  481.4 5.8 %reshape.204 = bf16[1536,1024]{1,0:T(8,128)(2,1)} reshape(bf16[3,8,512,128]{3,2,1,0:T(8,128)(2,1)} %get-tuple-element.32) | data formatting | bytes 6291456 | tf_op jit(solution)/shard_map/reshape | solution.py:93
  (47 shorter events, 1.8 us)
Async XLA Ops:
  6.5 102.3 %all-gather.2.cloned.1.call-start = ((), (), s32[]{:S(2)}) async-start(), calls=%async_computation.2 | async-start | bytes 17825792 | tf_op jit(solution)/shard_map/all_gather | solution.py:39
  12.7 14.0 %all-to-all-start = ((s32[16,1,32]{2,1,0:T(1,128)}), s32[16,1,32]{2,1,0:T(1,128)S(1)}, u32[]{:S(2)}, u32[]{:S(2)}) async-start(s32[16,1,32]{2,1,0:T(1,128)} %bitcast.6), calls=%async_computation | async-start | bytes 16384 | tf_op jit(solution)/shard_map/all_to_all | solution.py:50
  144.5 265.4 %all-to-all-start.1 = ((bf16[16,33,64,256]{3,2,1,0:T(8,128)(2,1)}), bf16[16,33,64,256]{3,2,1,0:T(8,128)(2,1)}, u32[]{:S(2)}, u32[]{:S(2)}) async-start(bf16[16,33,64,256]{3,2,1,0:T(8,128)(2,1)} %broadcast_select_fusion), calls=%async_computation.1 | async-start | bytes 34603008 | tf_op jit(solution)/shard_map/all_to_all | solution.py:60
  151.4 2.7 copy-start
Sparse Core Ops, SparseCore 0:
  9.2 99.6 all-gather.1
where the time goes:
time: 495 us; the launch traced here: 494 us
  waiting for transfers between devices  340 us (69%)
  local copies, waits for them, and re-layouts  62.3 us (13%)
  other arithmetic  43.8 us (9%)
  matrix products  20 us (4%)
  starting transfers between devices  14.2 us (3%)
  between operations  13.6 us (3%)
    all_to_all x1, waiting for transfers between devices, per_device(): lax.all_to_all(outgoing, 'kv', split_axis=0, concat_axis=0, tiled=True)  252 us
    all_gather x1, waiting for transfers between devices, per_device(): column = lax.all_gather(tiles_local, 'pb', axis=0, tiled=True)  82 us
    gather x3, local copies, waits for them, and re-layouts, attend(): jnp.take(tile_table, positions_in.reshape(-1), axis=0)  26.1 us
    gather x1, local copies, waits for them, and re-layouts, per_device(): jnp.take(column, picks.reshape(-1), axis=0)  21.2 us
    select_n x2, other arithmetic, per_device(): jnp.take(column, picks.reshape(-1), axis=0)  14.5 us
    select_n x6, other arithmetic, attend(): jnp.take(tile_table, positions_in.reshape(-1), axis=0)  13.8 us
    dot_general x3, matrix products, attend(): jnp.einsum('gqk,gkd->gqd', weights.astype(jnp.bfloat16), gathered[..., DH...  12.7 us
    reduce_sum x3, other arithmetic, attend(): totals = jnp.sum(weights, axis=-1, keepdims=True)  10.6 us
  transfers between devices with their start and end apart: 3, of which 3 were waited for; matrix products, arithmetic and copies ran while one was open for 2% of the time, Pallas kernels for 0%

commit v1 on v0

--- a/solution.py
+++ b/solution.py
@@ -10,6 +10,13 @@
 TOPN = 16
 QB = 64
 CAP = 2
+
+
+def swapped_in(x, name, along):
+    size = lax.axis_size(name)
+    parts = jnp.stack([x for _ in range(size)])
+    parts = lax.all_to_all(parts, name, split_axis=0, concat_axis=0)
+    return jnp.concatenate(parts, axis=along)
 
 
 def holdings(wanted, owner, blocks_here):
@@ -36,7 +43,7 @@
     tiles_local = jnp.concatenate(
         [keys.reshape(blocks_here, BLOCK, DH), values.reshape(blocks_here, BLOCK, DH)], axis=2
     )
-    column = lax.all_gather(tiles_local, "pb", axis=0, tiled=True)
+    column = swapped_in(tiles_local, "pb", 0)
     slots = CAP
     wanted = selected.reshape(-1)
     owners = jnp.arange(devices, dtype=jnp.int32)

time: 495 us -> 776 us (1.57)
  waiting for transfers between devices: 340 us -> 618 us
  between operations: 13.6 us -> 0.19 us
  starting transfers between devices: 14.2 us -> 23.3 us
    all_to_all x0 -> x1, waiting for transfers between devices: none -> 363 us  [swapped_in(): parts = lax.all_to_all(parts, name, split_axis=0, concat_axis=0)]
    all_gather x1 -> x0, waiting for transfers between devices: 82 us -> none  [per_device(): column = lax.all_gather(tiles_local, 'pb', axis=0, tiled=True)]
    all_to_all x0 -> x1, starting transfers between devices: none -> 10.6 us  [swapped_in(): parts = lax.all_to_all(parts, name, split_axis=0, concat_axis=0)]
  transfers between devices with their start and end apart: 3 -> 3, of which waited for: 3 -> 3; matrix products, arithmetic and copies ran while one was open for 2% -> 1% of each run, Pallas kernels for 0% -> 0%
where the time goes in v1:
time: 776 us; the launch traced here: 773 us
  waiting for transfers between devices  618 us (80%)
  local copies, waits for them, and re-layouts  68.2 us (9%)
  other arithmetic  42.8 us (6%)
  starting transfers between devices  23.3 us (3%)
  matrix products  20 us (3%)
    all_to_all x1, waiting for transfers between devices, swapped_in(): parts = lax.all_to_all(parts, name, split_axis=0, concat_axis=0)  363 us
    all_to_all x1, waiting for transfers between devices, per_device(): lax.all_to_all(outgoing, 'kv', split_axis=0, concat_axis=0, tiled=True)  250 us
    gather x3, local copies, waits for them, and re-layouts, attend(): jnp.take(tile_table, positions_in.reshape(-1), axis=0)  26.1 us
    gather x1, local copies, waits for them, and re-layouts, per_device(): jnp.take(column, picks.reshape(-1), axis=0)  21.2 us
  transfers between devices with their start and end apart: 3, of which 3 were waited for; matrix products, arithmetic and copies ran while one was open for 1% of the time, Pallas kernels for 0%

profile of v1, /device:TPU:1, one launch (start us, length us, event | category | flops | bytes accessed | tf_op | source)
XLA Modules:
  0.0 772.6 jit_solution(4852637744991415030)
XLA Ops:
  0.0 0.8 copy.30
  0.9 1.7 convert_reduce_fusion
  3.2 0.6 broadcast_add_fusion
  3.8 7.6 all-to-all-start
  11.4 1.3 pad_maximum_fusion
  12.7 5.0 all-to-all-done
  17.7 5.9 stack.2
  23.6 10.6 %all-to-all-start.1 = ((bf16[16,32,64,256]{3,2,1,0:T(8,128)(2,1)}), bf16[16,32,64,256]{3,2,1,0:T(8,128)(2,1)}, u32[]{:S(2)}, u32[]{:S(2)}) async-start(bf16[16,32,64,256]{3,2,1,0:T(8,128)(2,1)} %stack.2), calls=%async_computation.1 | async-start | bytes 33554432 | tf_op jit(solution)/shard_map/all_to_all | solution.py:18
  34.4 363.1 %all-to-all-done.1 = bf16[16,32,64,256]{3,2,1,0:T(8,128)(2,1)} async-done(((bf16[16,32,64,256]{3,2,1,0:T(8,128)(2,1)}), bf16[16,32,64,256]{3,2,1,0:T(8,128)(2,1)}, u32[]{:S(2)}, u32[]{:S(2)}) %all-to-all-start.1) | async-done | bytes 16777248 | tf_op jit(solution)/shard_map/all_to_all | solution.py:18
  397.5 21.2 %gather_fusion.2 = bf16[528,64,256]{2,1,0:T(8,128)(2,1)} fusion(bf16[512,64,256]{2,1,0:T(8,128)(2,1)} %bitcast.10, s32[1024]{0:T(1024)S(1)} %pad_clamp_fusion.1), kind=kCustom, calls=%fused_computation.2 | custom fusion | bytes 34605120 | tf_op jit(solution)/shard_map/jit(_take)/gather | solution.py:64
  418.7 14.4 %broadcast_select_fusion = bf16[16,33,64,256]{3,2,1,0:T(8,128)(2,1)} fusion(bf16[16,33,64,256]{3,2,1,0:T(8,128)(2,1)} %bitcast.38, pred[16,33]{1,0:T(8,128)(4,1)S(1)} %compare_and_fusion.1), kind=kLoop, calls=%fused_computation.26 | loop fusion | flops 8650752 | bytes 34603536 | tf_op jit(solution)/shard_map/jit(_take)/select_n | solution.py:64
  433.2 5.2 all-to-all-start.2
  438.7 2.5 gather_fusion.1
  441.3 4.1 reshape.202
  445.6 249.9 %all-to-all-done.2 = bf16[16,33,64,256]{3,2,1,0:T(8,128)(2,1)} async-done(((bf16[16,33,64,256]{3,2,1,0:T(8,128)(2,1)}), bf16[16,33,64,256]{3,2,1,0:T(8,128)(2,1)}, u32[]{:S(2)}, u32[]{:S(2)}) %all-to-all-start.2) | async-done | bytes 17301536 | tf_op jit(solution)/shard_map/all_to_all | solution.py:67
  695.5 71.4 %while.10 = (s32[]{:T(128)}, bf16[3,8,512,128]{3,2,1,0:T(8,128)(2,1)}, bf16[3,8,512,128]{3,2,1,0:T(8,128)(2,1)S(1)}, s32[3,8,16]{2,1,0:T(8,128)S(1)}, bf16[528,64,256]{2,1,0:T(8,128)(2,1)}, /*index=5*/s32[]{:T(128)}) while((s32[]{:T(128)}, bf16[3,8,512,128]{3,2,1,0:T(8,128)(2,1)}, bf16[3,8,512,128]{3,2,1,0:T(8,128)(2,1)S(1)}, ...), condition=%wide.region_6.7_spmd, body=%wide.region_3.6_spmd.sunk | while | flops 2184177664 | bytes 73524040 | solution.py:99
  695.6 8.7 %gather_fusion = bf16[128,64,256]{2,1,0:T(8,128)(2,1)} fusion(bf16[528,64,256]{2,1,0:T(8,128)(2,1)} %get-tuple-element.102, s32[1024]{0:T(1024)S(1)} %pad_clamp_fusion.4), kind=kCustom, calls=%fused_computation.clone.1 | custom fusion | bytes 8389120 | tf_op jit(solution)/shard_map/while/body/eval_jaxpr/jit(_take)/gather | solution.py:83
  704.5 4.6 bitcast_select_fusion.2
  709.1 2.4 multiply_reduce_fusion.2
  711.5 3.5 fusion.32
  715.0 4.3 bitcast_dynamic-update-slice_fusion.2
  719.4 8.7 %gather_fusion = bf16[128,64,256]{2,1,0:T(8,128)(2,1)} fusion(bf16[528,64,256]{2,1,0:T(8,128)(2,1)} %get-tuple-element.102, s32[1024]{0:T(1024)S(1)} %pad_clamp_fusion.4), kind=kCustom, calls=%fused_computation.clone.1 | custom fusion | bytes 8389120 | tf_op jit(solution)/shard_map/while/body/eval_jaxpr/jit(_take)/gather | solution.py:83
  728.3 4.6 bitcast_select_fusion.2
  732.9 2.4 multiply_reduce_fusion.2
  735.3 3.5 fusion.32
  738.8 4.2 bitcast_dynamic-update-slice_fusion.2
  743.2 8.7 %gather_fusion = bf16[128,64,256]{2,1,0:T(8,128)(2,1)} fusion(bf16[528,64,256]{2,1,0:T(8,128)(2,1)} %get-tuple-element.102, s32[1024]{0:T(1024)S(1)} %pad_clamp_fusion.4), kind=kCustom, calls=%fused_computation.clone.1 | custom fusion | bytes 8389120 | tf_op jit(solution)/shard_map/while/body/eval_jaxpr/jit(_take)/gather | solution.py:83
  752.1 4.6 bitcast_select_fusion.2
  756.6 2.4 multiply_reduce_fusion.2
  759.1 3.5 fusion.32
  762.6 4.2 bitcast_dynamic-update-slice_fusion.2
  766.9 5.8 reshape.210
  (47 shorter events, 2.1 us)
Async XLA Ops:
  3.8 13.9 %all-to-all-start = ((s32[16,1,32]{2,1,0:T(1,128)}), s32[16,1,32]{2,1,0:T(1,128)S(1)}, u32[]{:S(2)}, u32[]{:S(2)}) async-start(s32[16,1,32]{2,1,0:T(1,128)} %bitcast.6), calls=%async_computation | async-start | bytes 16384 | tf_op jit(solution)/shard_map/all_to_all | solution.py:57
  23.6 373.8 %all-to-all-start.1 = ((bf16[16,32,64,256]{3,2,1,0:T(8,128)(2,1)}), bf16[16,32,64,256]{3,2,1,0:T(8,128)(2,1)}, u32[]{:S(2)}, u32[]{:S(2)}) async-start(bf16[16,32,64,256]{3,2,1,0:T(8,128)(2,1)} %stack.2), calls=%async_computation.1 | async-start | bytes 33554432 | tf_op jit(solution)/shard_map/all_to_all | solution.py:18
  433.2 262.3 %all-to-all-start.2 = ((bf16[16,33,64,256]{3,2,1,0:T(8,128)(2,1)}), bf16[16,33,64,256]{3,2,1,0:T(8,128)(2,1)}, u32[]{:S(2)}, u32[]{:S(2)}) async-start(bf16[16,33,64,256]{3,2,1,0:T(8,128)(2,1)} %broadcast_select_fusion), calls=%async_computation.2 | async-start | bytes 34603008 | tf_op jit(solution)/shard_map/all_to_all | solution.py:67
  438.3 3.0 copy-start
